TPU v7x, 32 devices: a whole 2x2x4 slice. The times are simulated.
32 devices in a mesh: row: 8 (over z, core), col: 4 (over y, x).
Axes of the slice: x: 2, y: 2, z: 4, core: 2. Of those that a mesh axis runs over, the one named last changes fastest.
Arguments:
- amplitudes: bfloat16 [512, 512, 256], P('row', 'col'), may hold values from -6 to 6
- integrals: bfloat16 [512, 512, 256], P('row', 'col'), may hold values from -0.0625 to 0.0625
- occ_energy: float32 [16], replicated, may hold values from -1.5 to -0.5
- vir_energy: float32 [512], replicated, may hold values from 0.5 to 3
Outputs:
- updated: float32 [512, 512, 256], P('row', 'col')
All inputs are finite; a program needn't handle non-finite values.
Results may differ from a plain program's by a relative error of at most 0.0017.
Values may be sent and summed in bfloat16 or wider, within the bound.
No kernel may reach another device: no remote copies, remote signals or barrier semaphores. Data moves between devices by JAX's collectives and lax.ppermute only.
A program may use at most 192 MiB of HBM per device.

v0:
```python
import functools

import jax
import jax.numpy as jnp
import numpy as np
from jax import lax
from jax.experimental import pallas as pl
from jax.experimental.layout import Layout, with_layout_constraint
from jax.experimental.pallas import tpu as pltpu
from jax.sharding import PartitionSpec as P

OCC = 16
HALF = OCC // 2
CHUNKS = (12, 4)


def diff_kernel(first, earlier_firsts, *refs):
    current, earlier, out = refs[0], refs[1:-1], refs[-1]
    at = 0
    for j in range(first, first + current.shape[0]):
        sources = [(f, e.shape[0], e, first) for f, e in zip(earlier_firsts, earlier)]
        for begin, count, source, rows in sources + [(first, j - first, current, 0)]:
            if count == 0:
                continue

            def body(n, carry, begin=begin, source=source, rows=rows, j=j, at=at):
                out[at + n] = current[j - first, begin + n] - source[n, j - rows]
                return carry

            lax.fori_loop(0, count, body, 0)
            at += count


def diff_call(first, chunk, cycles, firsts):
    width, _, block_a, block_b = chunk.shape
    count = sum(range(first, first + width))
    shape = jax.ShapeDtypeStruct((count, block_a, block_b), jnp.float32)
    in_specs = [pl.BlockSpec(chunk.shape, lambda i: (0,) * 4)]
    for c in cycles:
        in_specs.append(pl.BlockSpec((c.shape[0], width, block_a, block_b),
                                     lambda i: (0, first // width, 0, 0)))
    return pl.pallas_call(
        functools.partial(diff_kernel, first, tuple(firsts)),
        grid=(1,), out_shape=shape, in_specs=in_specs, out_specs=pl.BlockSpec(shape.shape, lambda i: (0, 0, 0)),
        compiler_params=pltpu.CompilerParams(vmem_limit_bytes=40 * 1024 * 1024),
        cost_estimate=pl.CostEstimate(flops=count * block_a * block_b,
                                      bytes_accessed=count * block_a * block_b * 12, transcendentals=0),
    )(chunk, *cycles)


def resid_kernel(core_ref, diff_ref, near_ref, far_ref, out_ref):
    core = core_ref[0]
    block_a = near_ref.shape[1]
    row = lax.broadcasted_iota(jnp.int32, (block_a, 2 * block_a), 0)
    column = lax.broadcasted_iota(jnp.int32, (block_a, 2 * block_a), 1)
    pick = (column == row + core * block_a).astype(jnp.bfloat16)
    lower = core == 0

    def body(n, carry):
        near, far = near_ref[n], far_ref[n]
        rows = jnp.concatenate([jnp.where(lower, near, far), jnp.where(lower, far, near)], axis=0)
        turned = lax.dot_general(pick, rows, (((1,), (1,)), ((), ())), preferred_element_type=jnp.float32)
        out_ref[n] = diff_ref[n] - turned
        return carry

    lax.fori_loop(0, diff_ref.shape[0], body, 0)


def resid_call(core, diff, near, far):
    whole = lambda x: pl.BlockSpec(x.shape, lambda i, s: (0,) * x.ndim)
    return pl.pallas_call(
        resid_kernel, out_shape=jax.ShapeDtypeStruct(diff.shape, jnp.float32),
        grid_spec=pltpu.PrefetchScalarGridSpec(
            num_scalar_prefetch=1, grid=(1,), in_specs=[whole(diff), whole(near), whole(far)],
            out_specs=whole(diff)),
        compiler_params=pltpu.CompilerParams(vmem_limit_bytes=40 * 1024 * 1024),
        cost_estimate=pl.CostEstimate(flops=diff.size * 256, bytes_accessed=diff.size * 12, transcendentals=0),
    )(core.reshape(1), diff, near, far)


def turns_of(chips, cols):
    if chips == cols == 4:
        return [{(0, 3), (1, 2), (2, 3), (3, 0)}, {(2, 1), (1, 0)}]
    return []


def local(amplitudes, integrals, occ_energy, vir_energy, rows, cols):
    block_a, block_b, pair_count = amplitudes.shape
    chips = rows // 2
    row_pos = lax.axis_index("row")
    col_pos = lax.axis_index("col")
    core = row_pos % 2
    swap = [(r, r ^ 1) for r in range(rows)]

    def to_core(x):
        return lax.ppermute(x, "row", swap)

    def planes(x):
        return with_layout_constraint(x, Layout(major_to_minor=(0, 1, 2, 3)))

    ints = planes(integrals.reshape(block_a, block_b, OCC, OCC).transpose(2, 3, 0, 1))
    gathered, first = [], 0
    for width in CHUNKS:
        gathered.append(lax.all_gather(planes(ints[:, first:first + width]), "row", axis=2, tiled=True))
        first += width

    amps = planes(amplitudes.reshape(block_a, block_b, OCC, OCC).transpose(2, 3, 0, 1))

    def hop(x, bits):
        return lax.ppermute(x, "col", [(q, q ^ bits) for q in range(cols)])

    parts = (amps[:HALF], amps[HALF:])
    pieces = [parts]
    for step in range(1, cols):
        if step == 3:
            pieces.append((hop(pieces[1][0], 2), hop(pieces[2][1], 1)))
        else:
            pieces.append(tuple(hop(x, step) for x in parts))
    amp_all = jnp.zeros((OCC, OCC, block_a, cols * block_b), amps.dtype)
    for step, piece in enumerate(pieces):
        place = (col_pos ^ step) * block_b
        for n, part in enumerate([amps] if step == 0 else piece):
            amp_all = lax.dynamic_update_slice(amp_all, part, (n * HALF, 0, 0, place))

    at = lambda z, h, p: (z * 2 + h) * cols + p
    flows = [(z, h, p) for z in range(chips) for h in range(2) for p in range(cols)]
    turns = turns_of(chips, cols)
    direct = [(at(z, h, p), at(p, h, z)) for z, h, p in flows if not any((z, p) in t for t in turns)]

    def to_mirror(x):
        out = lax.ppermute(x, ("row", "col"), direct)
        for turn in turns:
            across = [(at(z, h, p), at(z, h, z)) for z, h, p in flows if (z, p) in turn]
            along = [(at(z, h, z), at(p, h, z)) for z, h, p in flows if (z, p) in turn]
            moved = lax.ppermute(x, ("row", "col"), across)
            out = out + lax.ppermute(moved, ("row", "col"), along)
        return out

    first, ready = 0, None
    cycles, firsts, resids, pairs = [], [], [], []
    for width, blocks in zip(CHUNKS, gathered):
        if ready is not None:
            blocks, _ = lax.optimization_barrier((blocks, ready))
        cycle = jnp.einsum("ikac,kjcb->jiab", amp_all, blocks, preferred_element_type=jnp.float32)
        diff = diff_call(first, cycle, cycles, firsts)
        cycles.append(cycle)
        firsts.append(first)
        pairs += [(i, j) for j in range(first, first + width) for i in range(j)]
        ready = diff.astype(jnp.bfloat16)
        near = to_mirror(ready)
        resids.append(resid_call(core, diff, near, to_core(near)))
        first += width

    expand = np.zeros((len(pairs), pair_count), np.float32)
    for at, (i, j) in enumerate(pairs):
        expand[at, i * OCC + j], expand[at, j * OCC + i] = 1, -1
    resid = jnp.concatenate(resids).transpose(1, 2, 0)
    full = jnp.einsum("abp,pq->abq", resid, jnp.asarray(expand), precision=lax.Precision.HIGHEST)

    vir_rows = lax.dynamic_slice_in_dim(vir_energy, row_pos * block_a, block_a)
    vir_cols = lax.dynamic_slice_in_dim(vir_energy, col_pos * block_b, block_b)
    denominator = (
        (occ_energy[:, None] + occ_energy[None, :]).reshape(1, 1, pair_count)
        - vir_rows[:, None, None]
        - vir_cols[None, :, None]
    )
    return amplitudes.astype(jnp.float32) + full / denominator


def solution(mesh):
    rows, cols = mesh.shape["row"], mesh.shape["col"]
    placed = (P("row", "col", None), P("row", "col", None), P(), P())

    def body(*args):
        return local(*args, rows, cols)

    return jax.shard_map(body, mesh=mesh, in_specs=placed, out_specs=P("row", "col", None), check_vma=False)
```

profile of v0, /device:TPU:0, one launch (start us, length us, event | category | flops | bytes accessed | tf_op | source)
XLA Modules:
  0.0 461.7 jit_solution(495854761449700891)
XLA Ops:
  6.5 6.4 %copy.7 = bf16[64,128,256]{1,0,2:T(8,128)(2,1)} copy(bf16[64,128,256]{2,1,0:T(8,128)(2,1)} %param.6) | data formatting | bytes 8388608 | tf_op args[1]
  13.0 4.5 slice.18
  17.5 2.3 slice.19
  19.9 6.5 %copy.6 = bf16[64,128,256]{1,0,2:T(8,128)(2,1)} copy(bf16[64,128,256]{2,1,0:T(8,128)(2,1)} %param.5) | data formatting | bytes 8388608 | tf_op args[0]
  26.3 6.2 %fusion.20 = (bf16[8,16,64,128]{3,2,1,0:T(8,128)(2,1)}, bf16[8,16,64,128]{3,2,1,0:T(8,128)(2,1)}) fusion(bf16[16,16,64,128]{3,2,1,0:T(8,128)(2,1)} %bitcast.37), kind=kLoop, calls=%fused_computation.23 | loop fusion | bytes 8388608 | tf_op jit(solution)/shard_map/slice | solution.py:112
  32.5 3.2 collective-permute-start
  35.7 1.5 collective-permute-start.3
  37.8 44.7 %collective-permute-done = bf16[8,16,64,128]{3,2,1,0:T(8,128)(2,1)} collective-permute-done((bf16[8,16,64,128]{3,2,1,0:T(8,128)(2,1)}, bf16[8,16,64,128]{3,2,1,0:T(8,128)(2,1)}, u32[]{:S(2)}, u32[]{:S(2)}) %collective-permute-start) | collective-permute-done | bytes 2097184 | tf_op jit(solution)/shard_map/ppermute | solution.py:110
  82.5 2.1 collective-permute-start.4
  84.6 1.5 collective-permute-start.5
  86.1 6.7 %broadcast_in_dim.2 = bf16[16,16,64,512]{3,2,1,0:T(8,128)(2,1)} broadcast(bf16[]{:T(256)} %constant.31.clone.1), dimensions={} | broadcast | bytes 16777218 | tf_op jit(solution)/shard_map/broadcast_in_dim | solution.py:119
  92.8 3.1 constant_dynamic-update-slice_fusion.6
  95.9 3.2 constant_dynamic-update-slice_fusion.5
  99.1 28.3 %collective-permute-done.1 = bf16[8,16,64,128]{3,2,1,0:T(8,128)(2,1)} collective-permute-done((bf16[8,16,64,128]{3,2,1,0:T(8,128)(2,1)}, bf16[8,16,64,128]{3,2,1,0:T(8,128)(2,1)}, u32[]{:S(2)}, u32[]{:S(2)}) %collective-permute-start.1) | collective-permute-done | bytes 2097184 | tf_op jit(solution)/shard_map/ppermute | solution.py:110
  127.4 3.2 constant_dynamic-update-slice_fusion.4
  130.7 3.2 constant_dynamic-update-slice_fusion.3
  133.9 1.7 constant_dynamic-update-slice_fusion.2
  135.6 37.3 %collective-permute-done.4 = bf16[8,16,64,128]{3,2,1,0:T(8,128)(2,1)} collective-permute-done((bf16[8,16,64,128]{3,2,1,0:T(8,128)(2,1)}, bf16[8,16,64,128]{3,2,1,0:T(8,128)(2,1)}, u32[]{:S(2)}, u32[]{:S(2)}) %collective-permute-start.4) | collective-permute-done | bytes 2097184 | tf_op jit(solution)/shard_map/ppermute | solution.py:110
  172.8 3.2 constant_dynamic-update-slice_fusion.1
  176.0 3.2 constant_dynamic-update-slice_fusion
  179.2 61.0 %all-gather.3.cloned.1.call-done = bf16[16,12,512,128]{3,2,1,0:T(8,128)(2,1)} async-done(((bf16[16,12,64,128]{3,2,1,0:T(8,128)(2,1)}), bf16[16,12,512,128]{3,2,1,0:T(8,128)(2,1)}) %all-gather.3.cloned.1.call-update) | async-done | bytes 25165840 | tf_op jit(solution)/shard_map/all_gather | solution.py:104
  240.2 31.2 %fusion.10.refs_0_.refs_1_ = f32[12,16,64,128]{3,2,1,0:T(8,128)S(1)} fusion(bf16[16,16,64,512]{3,2,1,0:T(8,128)(2,1)} %constant_dynamic-update-slice_fusion, bf16[16,12,512,128]{3,2,1,0:T(8,128)(2,1)} %all-gather.3.cloned.1.call-done), kind=kOutput, calls=%fused_computation.10 | convolution fusion | flops 25769803776 | bytes 48234496 | tf_op jit(solution)/shard_map/ikac,kjcb->jiab/dot_general | solution.py:144
  271.8 2.2 copy-done
  274.3 1.7 collective-permute-start.9
  276.0 1.3 collective-permute-start.7
  277.3 1.6 collective-permute-start.6
  278.9 62.2 %all-gather.5.cloned.1.call-done = bf16[16,4,512,128]{3,2,1,0:T(8,128)(2,1)} async-done(((bf16[16,4,64,128]{3,2,1,0:T(8,128)(2,1)}), bf16[16,4,512,128]{3,2,1,0:T(8,128)(2,1)}) %all-gather.5.cloned.1.call-update) | async-done | bytes 8388624 | tf_op jit(solution)/shard_map/all_gather | solution.py:104
  341.1 16.0 %fusion.15.refs_0_ = f32[4,16,64,128]{3,2,1,0:T(8,128)} fusion(bf16[16,16,64,512]{3,2,1,0:T(8,128)(2,1)} %constant_dynamic-update-slice_fusion, bf16[16,4,512,128]{3,2,1,0:T(8,128)(2,1)} %all-gather.5.cloned.1.call-done), kind=kOutput, calls=%fused_computation.11 | convolution fusion | flops 8589934592 | bytes 27262976 | tf_op jit(solution)/shard_map/ikac,kjcb->jiab/dot_general | solution.py:144
  357.1 2.8 copy-done.1
  359.9 1.6 copy-done.4
  362.1 1.4 collective-permute-start.13
  363.6 0.7 collective-permute-start.15
  364.3 0.7 collective-permute-start.10
  365.0 6.2 %collective-permute-start.8 = (bf16[66,64,128]{2,1,0:T(8,128)(2,1)}, bf16[66,64,128]{2,1,0:T(8,128)(2,1)S(1)}, u32[]{:S(2)}, u32[]{:S(2)}) collective-permute-start(bf16[66,64,128]{2,1,0:T(8,128)(2,1)} %collective-permute-done.7), channel_id=1, source_target_pairs={{0,24},{4,28},{9,17},{13,21},{18,26},{22,30},{27,3},{31,7}} | collective-permute-start | bytes 3244040 | tf_op jit(solution)/shard_map/ppermute | solution.py:136
  371.3 15.6 %collective-permute-done.13 = bf16[54,64,128]{2,1,0:T(8,128)(2,1)S(1)} collective-permute-done((bf16[54,64,128]{2,1,0:T(8,128)(2,1)S(1)}, bf16[54,64,128]{2,1,0:T(8,128)(2,1)S(1)}, u32[]{:S(2)}, u32[]{:S(2)}) %collective-permute-start.13) | collective-permute-done | bytes 884768 | tf_op jit(solution)/shard_map/ppermute | solution.py:135
  386.8 0.7 collective-permute-start.12
  387.6 2.1 collective-permute-start.14
  389.7 0.7 collective-permute-start.16
  390.5 5.3 %collective-permute-done.8 = bf16[66,64,128]{2,1,0:T(8,128)(2,1)S(1)} collective-permute-done((bf16[66,64,128]{2,1,0:T(8,128)(2,1)}, bf16[66,64,128]{2,1,0:T(8,128)(2,1)S(1)}, u32[]{:S(2)}, u32[]{:S(2)}) %collective-permute-start.8) | collective-permute-done | bytes 1081376 | tf_op jit(solution)/shard_map/ppermute | solution.py:136
  395.7 1.4 add_add_fusion.near_ref
  397.2 16.4 %collective-permute-done.14 = bf16[54,64,128]{2,1,0:T(8,128)(2,1)S(1)} collective-permute-done((bf16[54,64,128]{2,1,0:T(8,128)(2,1)S(1)}, bf16[54,64,128]{2,1,0:T(8,128)(2,1)S(1)}, u32[]{:S(2)}, u32[]{:S(2)}) %collective-permute-start.14) | collective-permute-done | bytes 884768 | tf_op jit(solution)/shard_map/ppermute | solution.py:136
  413.6 1.0 add_add_fusion.1.near_ref
  415.0 2.4 collective-permute-done.17.far_ref
  417.4 1.5 copy-done.3
  418.9 9.8 %shard_map.58 = f32[54,64,128]{2,1,0:T(8,128)S(1)} custom-call(s32[1]{0:T(128)} %bitcast.core_ref, f32[54,64,128]{2,1,0:T(8,128)S(1)} %copy-done.3, bf16[54,64,128]{2,1,0:T(8,128)(2,1)} %add_add_fusion.1.near_ref, bf16[54,64,128]{2,1,0:T(8,128)(2,1)} %collective-permute-done.17.far_ref), custom_call_target="tpu_custom_call" | custom-call | flops 113246208 | bytes 5308416 | tf_op jit(solution)/shard_map/pallas_call | solution.py:71
  428.6 11.5 %shard_map.56 = f32[66,64,128]{2,1,0:T(8,128)S(1)} custom-call(s32[1]{0:T(128)} %bitcast.core_ref, f32[66,64,128]{2,1,0:T(8,128)S(1)} %shard_map.55.diff_ref, bf16[66,64,128]{2,1,0:T(8,128)(2,1)S(1)} %add_add_fusion.near_ref, bf16[66,64,128]{2,1,0:T(8,128)(2,1)} %collective-permute-done.11.far_ref), custom_call_target="tpu_custom_call" | custom-call | flops 138412032 | bytes 6488064 | tf_op jit(solution)/shard_map/pallas_call | solution.py:71
  440.4 1.9 copy-done.6
  442.3 12.5 %divide_add_fusion = f32[64,128,256]{2,1,0:T(8,128)} fusion(bf16[64,128,256]{2,1,0:T(8,128)(2,1)S(1)} %copy-done.6, f32[128]{0:T(128)S(1)} %dynamic_slice.7, f32[64,256]{1,0:T(8,128)S(1)} %broadcast_subtract_fusion, f32[120,256,1]{1,0,2:T(8,128)S(1)} %copy-done.9, f32[64,128,120]{1,0,2:T(8,128)S(1)} %maximum_bitcast_fusion), kind=kOutput, calls=%fused_computation.6 | convolution fusion | flops 3028287488 | bytes 16704000 | tf_op jit(solution)/shard_map/abp,pq->abq/dot_general | solution.py:158
  (44 shorter events, 2.7 us)
Async XLA Ops:
  6.5 233.7 %all-gather.3.cloned.1.call-start = ((), (), s32[]{:S(2)}) async-start(), calls=%async_computation | async-start | bytes 28311552 | tf_op jit(solution)/shard_map/all_gather | solution.py:104
  17.5 323.6 %all-gather.5.cloned.1.call-start = ((), (), s32[]{:S(2)}) async-start(), calls=%async_computation.1 | async-start | bytes 9437184 | tf_op jit(solution)/shard_map/all_gather | solution.py:104
  32.5 50.0 %collective-permute-start = (bf16[8,16,64,128]{3,2,1,0:T(8,128)(2,1)}, bf16[8,16,64,128]{3,2,1,0:T(8,128)(2,1)}, u32[]{:S(2)}, u32[]{:S(2)}) collective-permute-start(bf16[8,16,64,128]{3,2,1,0:T(8,128)(2,1)} %get-tuple-element.8), channel_id=1, source_target_pairs={{0,1},{1,0},{2,3},{3,2},{4,5},{5,4},{6,7},{7,6},{8,9},{9,8},{10,11... | collective-permute-start | bytes 6291464 | tf_op jit(solution)/shard_map/ppermute | solution.py:110
  35.7 48.9 %collective-permute-start.3 = (bf16[8,16,64,128]{3,2,1,0:T(8,128)(2,1)}, bf16[8,16,64,128]{3,2,1,0:T(8,128)(2,1)S(1)}, u32[]{:S(2)}, u32[]{:S(2)}) collective-permute-start(bf16[8,16,64,128]{3,2,1,0:T(8,128)(2,1)} %get-tuple-element.7), channel_id=1, source_target_pairs={{0,2},{1,3},{2,0},{3,1},{4,6},{5,7},{6,4},{7,5},{8,10},{9,11},{10,... | collective-permute-start | bytes 6291464 | tf_op jit(solution)/shard_map/ppermute | solution.py:110
  37.2 90.2 %collective-permute-start.1 = (bf16[8,16,64,128]{3,2,1,0:T(8,128)(2,1)}, bf16[8,16,64,128]{3,2,1,0:T(8,128)(2,1)}, u32[]{:S(2)}, u32[]{:S(2)}) collective-permute-start(bf16[8,16,64,128]{3,2,1,0:T(8,128)(2,1)} %get-tuple-element.7), channel_id=1, source_target_pairs={{0,1},{1,0},{2,3},{3,2},{4,5},{5,4},{6,7},{7,6},{8,9},{9,8},{10,11... | collective-permute-start | bytes 6291464 | tf_op jit(solution)/shard_map/ppermute | solution.py:110
  37.8 92.9 %collective-permute-start.2 = (bf16[8,16,64,128]{3,2,1,0:T(8,128)(2,1)}, bf16[8,16,64,128]{3,2,1,0:T(8,128)(2,1)}, u32[]{:S(2)}, u32[]{:S(2)}) collective-permute-start(bf16[8,16,64,128]{3,2,1,0:T(8,128)(2,1)} %get-tuple-element.8), channel_id=1, source_target_pairs={{0,2},{1,3},{2,0},{3,1},{4,6},{5,7},{6,4},{7,5},{8,10},{9,11},{10,... | collective-permute-start | bytes 6291464 | tf_op jit(solution)/shard_map/ppermute | solution.py:110
  82.5 90.3 %collective-permute-start.4 = (bf16[8,16,64,128]{3,2,1,0:T(8,128)(2,1)}, bf16[8,16,64,128]{3,2,1,0:T(8,128)(2,1)}, u32[]{:S(2)}, u32[]{:S(2)}) collective-permute-start(bf16[8,16,64,128]{3,2,1,0:T(8,128)(2,1)} %collective-permute-done), channel_id=1, source_target_pairs={{0,2},{1,3},{2,0},{3,1},{4,6},{5,7},{6,4},{7,5},{8,10},{9,11},{10,... | collective-permute-start | bytes 6291464 | tf_op jit(solution)/shard_map/ppermute | solution.py:110
  84.6 91.4 %collective-permute-start.5 = (bf16[8,16,64,128]{3,2,1,0:T(8,128)(2,1)S(1)}, bf16[8,16,64,128]{3,2,1,0:T(8,128)(2,1)}, u32[]{:S(2)}, u32[]{:S(2)}) collective-permute-start(bf16[8,16,64,128]{3,2,1,0:T(8,128)(2,1)S(1)} %collective-permute-done.3), channel_id=1, source_target_pairs={{0,1},{1,0},{2,3},{3,2},{4,5},{5,4},{6,7},{7,6},{8,9},{9,8},{10,11... | collective-permute-start | bytes 6291464 | tf_op jit(solution)/shard_map/ppermute | solution.py:110
  86.1 6.7 %copy-start.5 = (bf16[64,128,256]{1,0,2:T(8,128)(2,1)S(1)}, bf16[64,128,256]{1,0,2:T(8,128)(2,1)}, u32[]{:S(2)}) copy-start(bf16[64,128,256]{1,0,2:T(8,128)(2,1)} %copy.6) | copy-start | bytes 12582916
  271.4 2.7 copy-start
  274.3 90.0 %collective-permute-start.9 = (bf16[66,64,128]{2,1,0:T(8,128)(2,1)S(1)}, bf16[66,64,128]{2,1,0:T(8,128)(2,1)}, u32[]{:S(2)}, u32[]{:S(2)}) collective-permute-start(bf16[66,64,128]{2,1,0:T(8,128)(2,1)S(1)} %convert_element_type.10), channel_id=1, source_target_pairs={{8,9},{12,13},{17,18},{21,22}} | collective-permute-start | bytes 3244040 | tf_op jit(solution)/shard_map/ppermute | solution.py:135
  276.0 89.1 %collective-permute-start.7 = (bf16[66,64,128]{2,1,0:T(8,128)(2,1)S(1)}, bf16[66,64,128]{2,1,0:T(8,128)(2,1)}, u32[]{:S(2)}, u32[]{:S(2)}) collective-permute-start(bf16[66,64,128]{2,1,0:T(8,128)(2,1)S(1)} %convert_element_type.10), channel_id=1, source_target_pairs={{3,0},{7,4},{10,9},{14,13},{19,18},{23,22},{24,27},{28,31}} | collective-permute-start | bytes 3244040 | tf_op jit(solution)/shard_map/ppermute | solution.py:135
  277.3 112.5 %collective-permute-start.6 = (bf16[66,64,128]{2,1,0:T(8,128)(2,1)S(1)}, bf16[66,64,128]{2,1,0:T(8,128)(2,1)}, u32[]{:S(2)}, u32[]{:S(2)}) collective-permute-start(bf16[66,64,128]{2,1,0:T(8,128)(2,1)S(1)} %convert_element_type.10), channel_id=1, source_target_pairs={{0,0},{1,8},{2,16},{4,4},{5,12},{6,20},{9,9},{11,25},{13,13},{15,2... | collective-permute-start | bytes 3244040 | tf_op jit(solution)/shard_map/ppermute | solution.py:131
  357.1 2.8 copy-start.1
  359.9 1.6 copy-start.4
  361.9 52.7 %copy-start.2 = (f32[54,64,128]{2,1,0:T(8,128)}, f32[54,64,128]{2,1,0:T(8,128)S(1)}, u32[]{:S(2)}) copy-start(f32[54,64,128]{2,1,0:T(8,128)S(1)} %shard_map.57.diff_ref) | copy-start | bytes 5308420
  362.1 52.5 %copy-start.8 = (f32[512]{0:T(512)S(1)}, f32[512]{0:T(512)}, u32[]{:S(2)}) copy-start(f32[512]{0:T(512)} %param.8) | copy-start | bytes 6148
  362.1 52.7 %copy-start.7 = (f32[16]{0:T(128)S(1)}, f32[16]{0:T(128)}, u32[]{:S(2)}) copy-start(f32[16]{0:T(128)} %param.7) | copy-start | bytes 196
  362.1 24.7 %collective-permute-start.13 = (bf16[54,64,128]{2,1,0:T(8,128)(2,1)S(1)}, bf16[54,64,128]{2,1,0:T(8,128)(2,1)S(1)}, u32[]{:S(2)}, u32[]{:S(2)}) collective-permute-start(bf16[54,64,128]{2,1,0:T(8,128)(2,1)S(1)} %convert_element_type.11), channel_id=1, source_target_pairs={{3,0},{7,4},{10,9},{14,13},{19,18},{23,22},{24,27},{28,31}} | collective-permute-start | bytes 2654216 | tf_op jit(solution)/shard_map/ppermute | solution.py:135
  363.6 24.0 %collective-permute-start.15 = (bf16[54,64,128]{2,1,0:T(8,128)(2,1)S(1)}, bf16[54,64,128]{2,1,0:T(8,128)(2,1)S(1)}, u32[]{:S(2)}, u32[]{:S(2)}) collective-permute-start(bf16[54,64,128]{2,1,0:T(8,128)(2,1)S(1)} %convert_element_type.11), channel_id=1, source_target_pairs={{8,9},{12,13},{17,18},{21,22}} | collective-permute-start | bytes 2654216 | tf_op jit(solution)/shard_map/ppermute | solution.py:135
  364.3 26.2 %collective-permute-start.10 = (bf16[66,64,128]{2,1,0:T(8,128)(2,1)}, bf16[66,64,128]{2,1,0:T(8,128)(2,1)S(1)}, u32[]{:S(2)}, u32[]{:S(2)}) collective-permute-start(bf16[66,64,128]{2,1,0:T(8,128)(2,1)} %collective-permute-done.9), channel_id=1, source_target_pairs={{9,1},{13,5},{18,10},{22,14}} | collective-permute-start | bytes 3244040 | tf_op jit(solution)/shard_map/ppermute | solution.py:136
  365.0 30.7 %collective-permute-start.8 = (bf16[66,64,128]{2,1,0:T(8,128)(2,1)}, bf16[66,64,128]{2,1,0:T(8,128)(2,1)S(1)}, u32[]{:S(2)}, u32[]{:S(2)}) collective-permute-start(bf16[66,64,128]{2,1,0:T(8,128)(2,1)} %collective-permute-done.7), channel_id=1, source_target_pairs={{0,24},{4,28},{9,17},{13,21},{18,26},{22,30},{27,3},{31,7}} | collective-permute-start | bytes 3244040 | tf_op jit(solution)/shard_map/ppermute | solution.py:136
  386.8 10.4 %collective-permute-start.12 = (bf16[54,64,128]{2,1,0:T(8,128)(2,1)S(1)}, bf16[54,64,128]{2,1,0:T(8,128)(2,1)S(1)}, u32[]{:S(2)}, u32[]{:S(2)}) collective-permute-start(bf16[54,64,128]{2,1,0:T(8,128)(2,1)S(1)} %convert_element_type.11), channel_id=1, source_target_pairs={{0,0},{1,8},{2,16},{4,4},{5,12},{6,20},{9,9},{11,25},{13,13},{15,2... | collective-permute-start | bytes 2654216 | tf_op jit(solution)/shard_map/ppermute | solution.py:131
  387.6 26.0 %collective-permute-start.14 = (bf16[54,64,128]{2,1,0:T(8,128)(2,1)S(1)}, bf16[54,64,128]{2,1,0:T(8,128)(2,1)S(1)}, u32[]{:S(2)}, u32[]{:S(2)}) collective-permute-start(bf16[54,64,128]{2,1,0:T(8,128)(2,1)S(1)} %collective-permute-done.13), channel_id=1, source_target_pairs={{0,24},{4,28},{9,17},{13,21},{18,26},{22,30},{27,3},{31,7}} | collective-permute-start | bytes 2654216 | tf_op jit(solution)/shard_map/ppermute | solution.py:136
  389.7 23.9 %collective-permute-start.16 = (bf16[54,64,128]{2,1,0:T(8,128)(2,1)S(1)}, bf16[54,64,128]{2,1,0:T(8,128)(2,1)S(1)}, u32[]{:S(2)}, u32[]{:S(2)}) collective-permute-start(bf16[54,64,128]{2,1,0:T(8,128)(2,1)S(1)} %collective-permute-done.15), channel_id=1, source_target_pairs={{9,1},{13,5},{18,10},{22,14}} | collective-permute-start | bytes 2654216 | tf_op jit(solution)/shard_map/ppermute | solution.py:136
  397.1 31.5 %collective-permute-start.11 = (bf16[66,64,128]{2,1,0:T(8,128)(2,1)S(1)}, bf16[66,64,128]{2,1,0:T(8,128)(2,1)}, u32[]{:S(2)}, u32[]{:S(2)}) collective-permute-start(bf16[66,64,128]{2,1,0:T(8,128)(2,1)S(1)} %add_add_fusion.near_ref), channel_id=1, source_target_pairs={{0,4},{4,0},{8,12},{12,8},{16,20},{20,16},{24,28},{28,24},{1,5},{5... | collective-permute-start | bytes 3244040 | tf_op jit(solution)/shard_map/ppermute | solution.py:96
  414.6 2.8 collective-permute-start.17
  417.4 1.5 copy-start.3
  440.1 2.2 copy-start.6
  440.1 2.2 copy-start.9
Sparse Core Ops, SparseCore 0:
  17.6 222.5 all-gather.2
  241.8 99.2 all-gather.4
where the time goes:
time: 465 us; the launch traced here: 462 us
  waiting for transfers between devices  273 us (59%)
  local copies, waits for them, and re-layouts  63.7 us (14%)
  matrix products  59.6 us (13%)
  starting transfers between devices  26.1 us (6%)
  Pallas kernels  22.1 us (5%)
  between operations  13.6 us (3%)
    all_gather x2, waiting for transfers between devices, local(): lax.all_gather(planes(ints[:, first:first + width]), 'row', axis=2, tiled...  123 us
    ppermute x6, waiting for transfers between devices, hop(): return lax.ppermute(x, 'col', [(q, q ^ bits) for q in range(cols)])  110 us
    dot_general x2, matrix products, local(): jnp.einsum('ikac,kjcb->jiab', amp_all, blocks, preferred_element_type=jnp...  47.1 us
    unnamed x22, local copies, waits for them, and re-layouts  22.9 us
    ppermute x4, waiting for transfers between devices, to_mirror(): out = out + lax.ppermute(moved, ('row', 'col'), along)  21.6 us
    pallas_call x2, Pallas kernels, resid_call(): pl.pallas_call(resid_kernel, out_shape=jax.ShapeDtypeStruct(diff.shape, j...  21.2 us
    dynamic_update_slice x7, local copies, waits for them, and re-layouts, local(): amp_all = lax.dynamic_update_slice(amp_all, part, (n * HALF, 0, 0, place))  20.8 us
    ppermute x4, waiting for transfers between devices, to_mirror(): moved = lax.ppermute(x, ('row', 'col'), across)  15.6 us
  transfers between devices with their start and end apart: 20, of which 9 were waited for; matrix products, arithmetic and copies ran while one was open for 20% of the time, Pallas kernels for 2%

commit v1 on v0

--- a/solution.py
+++ b/solution.py
@@ -11,20 +11,22 @@
 
 OCC = 16
 HALF = OCC // 2
-CHUNKS = (12, 4)
+CHUNKS = (14, 2)
 
 
 def diff_kernel(first, earlier_firsts, *refs):
-    current, earlier, out = refs[0], refs[1:-1], refs[-1]
+    current, earlier, out, sent = refs[0], refs[1:-2], refs[-2], refs[-1]
     at = 0
     for j in range(first, first + current.shape[0]):
-        sources = [(f, e.shape[0], e, first) for f, e in zip(earlier_firsts, earlier)]
+        sources = [(f, e.shape[0], e, first if e.shape[1] < OCC else 0) for f, e in zip(earlier_firsts, earlier)]
         for begin, count, source, rows in sources + [(first, j - first, current, 0)]:
             if count == 0:
                 continue
 
             def body(n, carry, begin=begin, source=source, rows=rows, j=j, at=at):
-                out[at + n] = current[j - first, begin + n] - source[n, j - rows]
+                value = current[j - first, begin + n] - source[n, j - rows]
+                out[at + n] = value
+                sent[at + n] = value.astype(sent.dtype)
                 return carry
 
             lax.fori_loop(0, count, body, 0)
@@ -36,15 +38,17 @@
     count = sum(range(first, first + width))
     shape = jax.ShapeDtypeStruct((count, block_a, block_b), jnp.float32)
     in_specs = [pl.BlockSpec(chunk.shape, lambda i: (0,) * 4)]
+    aligned = first % width == 0
     for c in cycles:
-        in_specs.append(pl.BlockSpec((c.shape[0], width, block_a, block_b),
-                                     lambda i: (0, first // width, 0, 0)))
+        in_specs.append(pl.BlockSpec((c.shape[0], width if aligned else OCC, block_a, block_b),
+                                     lambda i: (0, first // width if aligned else 0, 0, 0)))
     return pl.pallas_call(
         functools.partial(diff_kernel, first, tuple(firsts)),
-        grid=(1,), out_shape=shape, in_specs=in_specs, out_specs=pl.BlockSpec(shape.shape, lambda i: (0, 0, 0)),
+        grid=(1,), out_shape=(shape, jax.ShapeDtypeStruct(shape.shape, jnp.bfloat16)), in_specs=in_specs,
+        out_specs=(pl.BlockSpec(shape.shape, lambda i: (0, 0, 0)),) * 2,
         compiler_params=pltpu.CompilerParams(vmem_limit_bytes=40 * 1024 * 1024),
         cost_estimate=pl.CostEstimate(flops=count * block_a * block_b,
-                                      bytes_accessed=count * block_a * block_b * 12, transcendentals=0),
+                                      bytes_accessed=count * block_a * block_b * 14, transcendentals=0),
     )(chunk, *cycles)
 
 
@@ -56,14 +60,22 @@
     pick = (column == row + core * block_a).astype(jnp.bfloat16)
     lower = core == 0
 
-    def body(n, carry):
+    def turn(n):
         near, far = near_ref[n], far_ref[n]
         rows = jnp.concatenate([jnp.where(lower, near, far), jnp.where(lower, far, near)], axis=0)
         turned = lax.dot_general(pick, rows, (((1,), (1,)), ((), ())), preferred_element_type=jnp.float32)
         out_ref[n] = diff_ref[n] - turned
+
+    count, together = diff_ref.shape[0], 6
+
+    def body(n, carry):
+        for m in range(together):
+            turn(n * together + m)
         return carry
 
-    lax.fori_loop(0, diff_ref.shape[0], body, 0)
+    lax.fori_loop(0, count // together, body, 0)
+    for n in range(count - count % together, count):
+        turn(n)
 
 
 def resid_call(core, diff, near, far):
@@ -124,32 +136,35 @@
 
     at = lambda z, h, p: (z * 2 + h) * cols + p
     flows = [(z, h, p) for z in range(chips) for h in range(2) for p in range(cols)]
-    turns = turns_of(chips, cols)
-    direct = [(at(z, h, p), at(p, h, z)) for z, h, p in flows if not any((z, p) in t for t in turns)]
 
-    def to_mirror(x):
-        out = lax.ppermute(x, ("row", "col"), direct)
+    def to_mirror(x, at_chunk):
+        turns = turns_of(chips, cols) if at_chunk + 1 < len(CHUNKS) else []
+        direct = [(at(z, h, p), at(p, h, z)) for z, h, p in flows if not any((z, p) in t for t in turns)]
+        arrivals = [lax.ppermute(x, ("row", "col"), direct)]
         for turn in turns:
             across = [(at(z, h, p), at(z, h, z)) for z, h, p in flows if (z, p) in turn]
             along = [(at(z, h, z), at(p, h, z)) for z, h, p in flows if (z, p) in turn]
             moved = lax.ppermute(x, ("row", "col"), across)
-            out = out + lax.ppermute(moved, ("row", "col"), along)
-        return out
+            arrivals.append(lax.ppermute(moved, ("row", "col"), along))
+        return arrivals
 
     first, ready = 0, None
-    cycles, firsts, resids, pairs = [], [], [], []
-    for width, blocks in zip(CHUNKS, gathered):
+    cycles, firsts, mirrors, pairs = [], [], [], []
+    for at_chunk, (width, blocks) in enumerate(zip(CHUNKS, gathered)):
         if ready is not None:
             blocks, _ = lax.optimization_barrier((blocks, ready))
         cycle = jnp.einsum("ikac,kjcb->jiab", amp_all, blocks, preferred_element_type=jnp.float32)
-        diff = diff_call(first, cycle, cycles, firsts)
+        diff, ready = diff_call(first, cycle, cycles, firsts)
         cycles.append(cycle)
         firsts.append(first)
         pairs += [(i, j) for j in range(first, first + width) for i in range(j)]
-        ready = diff.astype(jnp.bfloat16)
-        near = to_mirror(ready)
+        mirrors.append((diff, to_mirror(ready, at_chunk)))
+        first += width
+
+    resids = []
+    for diff, arrivals in mirrors:
+        near = sum(arrivals[1:], arrivals[0])
         resids.append(resid_call(core, diff, near, to_core(near)))
-        first += width
 
     expand = np.zeros((len(pairs), pair_count), np.float32)
     for at, (i, j) in enumerate(pairs):

time: 465 us -> 468 us (level)
  the two profiles are of different devices: /device:TPU:0 before, /device:TPU:29 now
where the time goes in v1:
time: 468 us; the launch traced here: 467 us
  waiting for transfers between devices  294 us (63%)
  local copies, waits for them, and re-layouts  68.5 us (15%)
  matrix products  60.9 us (13%)
  starting transfers between devices  20.4 us (4%)
  between operations  13.6 us (3%)
  Pallas kernels  6.95 us (1%)
    ppermute x6, waiting for transfers between devices, hop(): return lax.ppermute(x, 'col', [(q, q ^ bits) for q in range(cols)])  111 us
    all_gather x2, waiting for transfers between devices, local(): lax.all_gather(planes(ints[:, first:first + width]), 'row', axis=2, tiled...  96.5 us
    ppermute x2, waiting for transfers between devices, to_mirror(): arrivals = [lax.ppermute(x, ('row', 'col'), direct)]  51.5 us
    dot_general x2, matrix products, local(): jnp.einsum('ikac,kjcb->jiab', amp_all, blocks, preferred_element_type=jnp...  48.4 us
    ppermute x2, waiting for transfers between devices, to_mirror(): arrivals.append(lax.ppermute(moved, ('row', 'col'), along))  33.9 us
    unnamed x26, local copies, waits for them, and re-layouts  27.7 us
    dynamic_update_slice x7, local copies, waits for them, and re-layouts, local(): amp_all = lax.dynamic_update_slice(amp_all, part, (n * HALF, 0, 0, place))  20.8 us
    dot_general x1, matrix products, local(): jnp.einsum('abp,pq->abq', resid, jnp.asarray(expand), precision=lax.Preci...  12.5 us
  transfers between devices with their start and end apart: 16, of which 9 were waited for; matrix products, arithmetic and copies ran while one was open for 19% of the time, Pallas kernels for 1%

profile of v1, /device:TPU:29, one launch (start us, length us, event | category | flops | bytes accessed | tf_op | source)
XLA Modules:
  0.0 466.7 jit_solution(13777175109862410477)
XLA Ops:
  6.5 6.6 %copy.7 = bf16[64,128,256]{1,0,2:T(8,128)(2,1)} copy(bf16[64,128,256]{2,1,0:T(8,128)(2,1)} %param.6) | data formatting | bytes 8388608 | tf_op args[1]
  13.1 5.1 %slice.18 = bf16[16,14,64,128]{3,2,1,0:T(8,128)(2,1)} slice(bf16[16,16,64,128]{3,2,1,0:T(8,128)(2,1)} %bitcast.39), slice={[0:16], [0:14], [0:64], [0:128]} | slice | bytes 7340032 | tf_op jit(solution)/shard_map/slice | solution.py:116
  18.3 6.5 %copy.6 = bf16[64,128,256]{1,0,2:T(8,128)(2,1)} copy(bf16[64,128,256]{2,1,0:T(8,128)(2,1)} %param.5) | data formatting | bytes 8388608 | tf_op args[0]
  24.7 6.1 %fusion.20 = (bf16[8,16,64,128]{3,2,1,0:T(8,128)(2,1)}, bf16[8,16,64,128]{3,2,1,0:T(8,128)(2,1)}) fusion(bf16[16,16,64,128]{3,2,1,0:T(8,128)(2,1)} %bitcast.37), kind=kLoop, calls=%fused_computation.22 | loop fusion | bytes 8388608 | tf_op jit(solution)/shard_map/slice | solution.py:124
  30.8 1.2 collective-permute-start
  32.5 1.3 collective-permute-start.2
  33.8 43.7 %collective-permute-done = bf16[8,16,64,128]{3,2,1,0:T(8,128)(2,1)} collective-permute-done((bf16[8,16,64,128]{3,2,1,0:T(8,128)(2,1)}, bf16[8,16,64,128]{3,2,1,0:T(8,128)(2,1)}, u32[]{:S(2)}, u32[]{:S(2)}) %collective-permute-start) | collective-permute-done | bytes 2097184 | tf_op jit(solution)/shard_map/ppermute | solution.py:122
  77.7 0.7 collective-permute-done.3
  78.4 0.5 collective-permute-start.5
  78.9 1.9 slice.19
  80.8 6.7 %broadcast_in_dim.2 = bf16[16,16,64,512]{3,2,1,0:T(8,128)(2,1)} broadcast(bf16[]{:T(256)} %constant.31.clone.1), dimensions={} | broadcast | bytes 16777218 | tf_op jit(solution)/shard_map/broadcast_in_dim | solution.py:131
  87.6 3.1 constant_dynamic-update-slice_fusion.6
  90.7 3.2 constant_dynamic-update-slice_fusion.5
  93.9 28.5 %collective-permute-done.1 = bf16[8,16,64,128]{3,2,1,0:T(8,128)(2,1)} collective-permute-done((bf16[8,16,64,128]{3,2,1,0:T(8,128)(2,1)}, bf16[8,16,64,128]{3,2,1,0:T(8,128)(2,1)}, u32[]{:S(2)}, u32[]{:S(2)}) %collective-permute-start.1) | collective-permute-done | bytes 2097184 | tf_op jit(solution)/shard_map/ppermute | solution.py:122
  122.4 3.3 constant_dynamic-update-slice_fusion.4
  125.7 3.2 constant_dynamic-update-slice_fusion.3
  128.8 1.7 constant_dynamic-update-slice_fusion.2
  130.5 37.7 %collective-permute-done.4 = bf16[8,16,64,128]{3,2,1,0:T(8,128)(2,1)} collective-permute-done((bf16[8,16,64,128]{3,2,1,0:T(8,128)(2,1)}, bf16[8,16,64,128]{3,2,1,0:T(8,128)(2,1)}, u32[]{:S(2)}, u32[]{:S(2)}) %collective-permute-start.4) | collective-permute-done | bytes 2097184 | tf_op jit(solution)/shard_map/ppermute | solution.py:122
  168.2 3.1 constant_dynamic-update-slice_fusion.1
  171.4 3.2 constant_dynamic-update-slice_fusion
  174.6 96.5 %all-gather.3.cloned.1.call-done = bf16[16,14,512,128]{3,2,1,0:T(8,128)(2,1)} async-done(((bf16[16,14,64,128]{3,2,1,0:T(8,128)(2,1)}), bf16[16,14,512,128]{3,2,1,0:T(8,128)(2,1)}) %all-gather.3.cloned.1.call-update) | async-done | bytes 29360144 | tf_op jit(solution)/shard_map/all_gather | solution.py:116
  271.1 35.9 %fusion.10.refs_0_.refs_1_ = f32[14,16,64,128]{3,2,1,0:T(8,128)S(1)} fusion(bf16[16,16,64,512]{3,2,1,0:T(8,128)(2,1)} %constant_dynamic-update-slice_fusion, bf16[16,14,512,128]{3,2,1,0:T(8,128)(2,1)} %all-gather.3.cloned.1.call-done), kind=kOutput, calls=%fused_computation.10 | convolution fusion | flops 30064771072 | bytes 53477376 | tf_op jit(solution)/shard_map/ikac,kjcb->jiab/dot_general | solution.py:156
  307.0 0.7 shard_map.55
  307.7 3.0 copy-done
  310.7 1.6 copy-done.2
  312.3 1.8 collective-permute-start.9
  314.1 1.8 collective-permute-start.7
  315.9 5.2 %collective-permute-start.6 = (bf16[91,64,128]{2,1,0:T(8,128)(2,1)S(1)}, bf16[91,64,128]{2,1,0:T(8,128)(2,1)S(1)}, u32[]{:S(2)}, u32[]{:S(2)}) collective-permute-start(bf16[91,64,128]{2,1,0:T(8,128)(2,1)S(1)} %get-tuple-element.11), channel_id=1, source_target_pairs={{0,0},{1,8},{2,16},{4,4},{5,12},{6,20},{9,9},{11,25},{13,13},{15,2... | collective-permute-start | bytes 4472840 | tf_op jit(solution)/shard_map/ppermute | solution.py:143
  321.1 1.8 collective-permute-start.10
  322.9 1.5 collective-permute-start.8
  324.4 28.0 %collective-permute-done.6 = bf16[91,64,128]{2,1,0:T(8,128)(2,1)S(1)} collective-permute-done((bf16[91,64,128]{2,1,0:T(8,128)(2,1)S(1)}, bf16[91,64,128]{2,1,0:T(8,128)(2,1)S(1)}, u32[]{:S(2)}, u32[]{:S(2)}) %collective-permute-start.6) | collective-permute-done | bytes 1490976 | tf_op jit(solution)/shard_map/ppermute | solution.py:143
  352.4 33.9 %collective-permute-done.8 = bf16[91,64,128]{2,1,0:T(8,128)(2,1)} collective-permute-done((bf16[91,64,128]{2,1,0:T(8,128)(2,1)}, bf16[91,64,128]{2,1,0:T(8,128)(2,1)}, u32[]{:S(2)}, u32[]{:S(2)}) %collective-permute-start.8) | collective-permute-done | bytes 1490976 | tf_op jit(solution)/shard_map/ppermute | solution.py:148
  386.3 2.0 add_add_fusion.near_ref
  388.4 1.8 collective-permute-start.11
  390.1 12.5 %fusion.15.refs_0_ = f32[2,16,64,128]{3,2,1,0:T(8,128)} fusion(bf16[16,16,64,512]{3,2,1,0:T(8,128)(2,1)} %constant_dynamic-update-slice_fusion, bf16[16,2,512,128]{3,2,1,0:T(8,128)(2,1)} %all-gather.5.cloned.1.call-done), kind=kOutput, calls=%fused_computation.12 | convolution fusion | flops 4294967296 | bytes 22020096 | tf_op jit(solution)/shard_map/ikac,kjcb->jiab/dot_general | solution.py:156
  402.7 3.1 copy-done.1
  405.7 1.2 copy-done.4
  407.3 0.9 copy-done.5
  408.2 1.9 collective-permute-start.12
  410.1 23.5 %collective-permute-done.12.near_ref = bf16[29,64,128]{2,1,0:T(8,128)(2,1)S(1)} collective-permute-done((bf16[29,64,128]{2,1,0:T(8,128)(2,1)S(1)}, bf16[29,64,128]{2,1,0:T(8,128)(2,1)S(1)}, u32[]{:S(2)}, u32[]{:S(2)}) %collective-permute-start.12) | collective-permute-done | bytes 475168 | tf_op jit(solution)/shard_map/ppermute | solution.py:143
  433.6 0.9 collective-permute-start.13
  434.8 1.2 collective-permute-done.13.far_ref
  436.0 1.2 copy-done.6
  437.2 2.2 shard_map.58
  439.5 1.8 copy-done.3
  441.3 3.8 shard_map.56
  445.6 1.7 copy-done.8
  447.3 12.5 %divide_add_fusion = f32[64,128,256]{2,1,0:T(8,128)} fusion(bf16[64,128,256]{2,1,0:T(8,128)(2,1)S(1)} %copy-done.8, f32[128]{0:T(128)S(1)} %dynamic_slice.7, f32[64,256]{1,0:T(8,128)S(1)} %broadcast_subtract_fusion, f32[120,256,1]{1,0,2:T(8,128)S(1)} %copy-done.11, f32[64,128,120]{1,0,2:T(8,128)S(1)} %maximum_bitcast_fusion), kind=kOutput, calls=%fused_computation.5 | convolution fusion | flops 3028287488 | bytes 16704000 | tf_op jit(solution)/shard_map/abp,pq->abq/dot_general | solution.py:173
  (37 shorter events, 2.0 us)
Async XLA Ops:
  6.5 264.6 %all-gather.3.cloned.1.call-start = ((), (), s32[]{:S(2)}) async-start(), calls=%async_computation | async-start | bytes 33030144 | tf_op jit(solution)/shard_map/all_gather | solution.py:116
  18.2 306.2 %all-gather.5.cloned.1.call-start = ((), (), s32[]{:S(2)}) async-start(), calls=%async_computation.1 | async-start | bytes 4718592 | tf_op jit(solution)/shard_map/all_gather | solution.py:116
  30.8 46.6 %collective-permute-start = (bf16[8,16,64,128]{3,2,1,0:T(8,128)(2,1)}, bf16[8,16,64,128]{3,2,1,0:T(8,128)(2,1)}, u32[]{:S(2)}, u32[]{:S(2)}) collective-permute-start(bf16[8,16,64,128]{3,2,1,0:T(8,128)(2,1)} %get-tuple-element.16), channel_id=1, source_target_pairs={{0,1},{1,0},{2,3},{3,2},{4,5},{5,4},{6,7},{7,6},{8,9},{9,8},{10,11... | collective-permute-start | bytes 6291464 | tf_op jit(solution)/shard_map/ppermute | solution.py:122
  32.1 46.3 %collective-permute-start.3 = (bf16[8,16,64,128]{3,2,1,0:T(8,128)(2,1)}, bf16[8,16,64,128]{3,2,1,0:T(8,128)(2,1)S(1)}, u32[]{:S(2)}, u32[]{:S(2)}) collective-permute-start(bf16[8,16,64,128]{3,2,1,0:T(8,128)(2,1)} %get-tuple-element.15), channel_id=1, source_target_pairs={{0,2},{1,3},{2,0},{3,1},{4,6},{5,7},{6,4},{7,5},{8,10},{9,11},{10,... | collective-permute-start | bytes 6291464 | tf_op jit(solution)/shard_map/ppermute | solution.py:122
  32.3 90.1 %collective-permute-start.1 = (bf16[8,16,64,128]{3,2,1,0:T(8,128)(2,1)}, bf16[8,16,64,128]{3,2,1,0:T(8,128)(2,1)}, u32[]{:S(2)}, u32[]{:S(2)}) collective-permute-start(bf16[8,16,64,128]{3,2,1,0:T(8,128)(2,1)} %get-tuple-element.15), channel_id=1, source_target_pairs={{0,1},{1,0},{2,3},{3,2},{4,5},{5,4},{6,7},{7,6},{8,9},{9,8},{10,11... | collective-permute-start | bytes 6291464 | tf_op jit(solution)/shard_map/ppermute | solution.py:122
  32.5 93.1 %collective-permute-start.2 = (bf16[8,16,64,128]{3,2,1,0:T(8,128)(2,1)}, bf16[8,16,64,128]{3,2,1,0:T(8,128)(2,1)}, u32[]{:S(2)}, u32[]{:S(2)}) collective-permute-start(bf16[8,16,64,128]{3,2,1,0:T(8,128)(2,1)} %get-tuple-element.16), channel_id=1, source_target_pairs={{0,2},{1,3},{2,0},{3,1},{4,6},{5,7},{6,4},{7,5},{8,10},{9,11},{10,... | collective-permute-start | bytes 6291464 | tf_op jit(solution)/shard_map/ppermute | solution.py:122
  77.4 90.8 %collective-permute-start.4 = (bf16[8,16,64,128]{3,2,1,0:T(8,128)(2,1)}, bf16[8,16,64,128]{3,2,1,0:T(8,128)(2,1)}, u32[]{:S(2)}, u32[]{:S(2)}) collective-permute-start(bf16[8,16,64,128]{3,2,1,0:T(8,128)(2,1)} %collective-permute-done), channel_id=1, source_target_pairs={{0,2},{1,3},{2,0},{3,1},{4,6},{5,7},{6,4},{7,5},{8,10},{9,11},{10,... | collective-permute-start | bytes 6291464 | tf_op jit(solution)/shard_map/ppermute | solution.py:122
  78.4 93.0 %collective-permute-start.5 = (bf16[8,16,64,128]{3,2,1,0:T(8,128)(2,1)S(1)}, bf16[8,16,64,128]{3,2,1,0:T(8,128)(2,1)}, u32[]{:S(2)}, u32[]{:S(2)}) collective-permute-start(bf16[8,16,64,128]{3,2,1,0:T(8,128)(2,1)S(1)} %collective-permute-done.3), channel_id=1, source_target_pairs={{0,1},{1,0},{2,3},{3,2},{4,5},{5,4},{6,7},{7,6},{8,9},{9,8},{10,11... | collective-permute-start | bytes 6291464 | tf_op jit(solution)/shard_map/ppermute | solution.py:122
  80.8 6.8 %copy-start.7 = (bf16[64,128,256]{1,0,2:T(8,128)(2,1)S(1)}, bf16[64,128,256]{1,0,2:T(8,128)(2,1)}, u32[]{:S(2)}) copy-start(bf16[64,128,256]{1,0,2:T(8,128)(2,1)} %copy.6) | copy-start | bytes 12582916
  307.7 3.1 copy-start
  310.7 1.6 copy-start.2
  312.3 8.8 %collective-permute-start.9 = (bf16[91,64,128]{2,1,0:T(8,128)(2,1)S(1)}, bf16[91,64,128]{2,1,0:T(8,128)(2,1)}, u32[]{:S(2)}, u32[]{:S(2)}) collective-permute-start(bf16[91,64,128]{2,1,0:T(8,128)(2,1)S(1)} %get-tuple-element.11), channel_id=1, source_target_pairs={{8,9},{12,13},{17,18},{21,22}} | collective-permute-start | bytes 4472840 | tf_op jit(solution)/shard_map/ppermute | solution.py:147
  314.1 8.8 %collective-permute-start.7 = (bf16[91,64,128]{2,1,0:T(8,128)(2,1)S(1)}, bf16[91,64,128]{2,1,0:T(8,128)(2,1)}, u32[]{:S(2)}, u32[]{:S(2)}) collective-permute-start(bf16[91,64,128]{2,1,0:T(8,128)(2,1)S(1)} %get-tuple-element.11), channel_id=1, source_target_pairs={{3,0},{7,4},{10,9},{14,13},{19,18},{23,22},{24,27},{28,31}} | collective-permute-start | bytes 4472840 | tf_op jit(solution)/shard_map/ppermute | solution.py:147
  315.9 36.6 %collective-permute-start.6 = (bf16[91,64,128]{2,1,0:T(8,128)(2,1)S(1)}, bf16[91,64,128]{2,1,0:T(8,128)(2,1)S(1)}, u32[]{:S(2)}, u32[]{:S(2)}) collective-permute-start(bf16[91,64,128]{2,1,0:T(8,128)(2,1)S(1)} %get-tuple-element.11), channel_id=1, source_target_pairs={{0,0},{1,8},{2,16},{4,4},{5,12},{6,20},{9,9},{11,25},{13,13},{15,2... | collective-permute-start | bytes 4472840 | tf_op jit(solution)/shard_map/ppermute | solution.py:143
  321.1 31.3 %collective-permute-start.10 = (bf16[91,64,128]{2,1,0:T(8,128)(2,1)}, bf16[91,64,128]{2,1,0:T(8,128)(2,1)}, u32[]{:S(2)}, u32[]{:S(2)}) collective-permute-start(bf16[91,64,128]{2,1,0:T(8,128)(2,1)} %collective-permute-done.9), channel_id=1, source_target_pairs={{9,1},{13,5},{18,10},{22,14}} | collective-permute-start | bytes 4472840 | tf_op jit(solution)/shard_map/ppermute | solution.py:148
  322.9 63.4 %collective-permute-start.8 = (bf16[91,64,128]{2,1,0:T(8,128)(2,1)}, bf16[91,64,128]{2,1,0:T(8,128)(2,1)}, u32[]{:S(2)}, u32[]{:S(2)}) collective-permute-start(bf16[91,64,128]{2,1,0:T(8,128)(2,1)} %collective-permute-done.7), channel_id=1, source_target_pairs={{0,24},{4,28},{9,17},{13,21},{18,26},{22,30},{27,3},{31,7}} | collective-permute-start | bytes 4472840 | tf_op jit(solution)/shard_map/ppermute | solution.py:148
  388.4 51.1 %collective-permute-start.11 = (bf16[91,64,128]{2,1,0:T(8,128)(2,1)S(1)}, bf16[91,64,128]{2,1,0:T(8,128)(2,1)S(1)}, u32[]{:S(2)}, u32[]{:S(2)}) collective-permute-start(bf16[91,64,128]{2,1,0:T(8,128)(2,1)S(1)} %add_add_fusion.near_ref), channel_id=1, source_target_pairs={{0,4},{4,0},{8,12},{12,8},{16,20},{20,16},{24,28},{28,24},{1,5},{5... | collective-permute-start | bytes 4472840 | tf_op jit(solution)/shard_map/ppermute | solution.py:108
  402.7 3.1 copy-start.1
  405.7 1.2 copy-start.4
  407.0 27.5 %copy-start.10 = (f32[512]{0:T(512)S(1)}, f32[512]{0:T(512)}, u32[]{:S(2)}) copy-start(f32[512]{0:T(512)} %param.8) | copy-start | bytes 6148
  407.0 27.6 %copy-start.9 = (f32[16]{0:T(128)S(1)}, f32[16]{0:T(128)}, u32[]{:S(2)}) copy-start(f32[16]{0:T(128)} %param.7) | copy-start | bytes 196
  407.3 0.9 copy-start.5
  408.2 25.4 %collective-permute-start.12 = (bf16[29,64,128]{2,1,0:T(8,128)(2,1)S(1)}, bf16[29,64,128]{2,1,0:T(8,128)(2,1)S(1)}, u32[]{:S(2)}, u32[]{:S(2)}) collective-permute-start(bf16[29,64,128]{2,1,0:T(8,128)(2,1)S(1)} %get-tuple-element.14), channel_id=1, source_target_pairs={{0,0},{1,8},{2,16},{3,24},{4,4},{5,12},{6,20},{7,28},{8,1},{9,9},{... | collective-permute-start | bytes 1425416 | tf_op jit(solution)/shard_map/ppermute | solution.py:143
  433.6 2.5 collective-permute-start.13
  436.0 1.2 copy-start.6
  439.5 1.8 copy-start.3
  445.1 2.2 copy-start.8
  445.1 2.2 copy-start.11
Sparse Core Ops, SparseCore 0:
  18.3 252.7 all-gather.2
  272.7 45.6 all-gather.4

commit v2 on v1

--- a/solution.py
+++ b/solution.py
@@ -11,7 +11,8 @@
 
 OCC = 16
 HALF = OCC // 2
-CHUNKS = (14, 2)
+GATHERS = (14, 2)
+CHUNKS = (11, 3, 2)
 
 
 def diff_kernel(first, earlier_firsts, *refs):
@@ -112,8 +113,9 @@
 
     ints = planes(integrals.reshape(block_a, block_b, OCC, OCC).transpose(2, 3, 0, 1))
     gathered, first = [], 0
-    for width in CHUNKS:
-        gathered.append(lax.all_gather(planes(ints[:, first:first + width]), "row", axis=2, tiled=True))
+    for width in GATHERS:
+        gathered.append(
+            (first, lax.all_gather(planes(ints[:, first:first + width]), "row", axis=2, tiled=True)))
         first += width
 
     amps = planes(amplitudes.reshape(block_a, block_b, OCC, OCC).transpose(2, 3, 0, 1))
@@ -150,10 +152,12 @@
 
     first, ready = 0, None
     cycles, firsts, mirrors, pairs = [], [], [], []
-    for at_chunk, (width, blocks) in enumerate(zip(CHUNKS, gathered)):
+    for at_chunk, width in enumerate(CHUNKS):
+        begin, blocks = [g for g in gathered if g[0] <= first][-1]
         if ready is not None:
             blocks, _ = lax.optimization_barrier((blocks, ready))
-        cycle = jnp.einsum("ikac,kjcb->jiab", amp_all, blocks, preferred_element_type=jnp.float32)
+        cycle = jnp.einsum("ikac,kjcb->jiab", amp_all, blocks[:, first - begin:first - begin + width],
+                           preferred_element_type=jnp.float32)
         diff, ready = diff_call(first, cycle, cycles, firsts)
         cycles.append(cycle)
         firsts.append(first)
@@ -170,7 +174,7 @@
     for at, (i, j) in enumerate(pairs):
         expand[at, i * OCC + j], expand[at, j * OCC + i] = 1, -1
     resid = jnp.concatenate(resids).transpose(1, 2, 0)
-    full = jnp.einsum("abp,pq->abq", resid, jnp.asarray(expand), precision=lax.Precision.HIGHEST)
+    full = jnp.einsum("abp,pq->abq", resid, jnp.asarray(expand), precision=lax.Precision.HIGH)
 
     vir_rows = lax.dynamic_slice_in_dim(vir_energy, row_pos * block_a, block_a)
     vir_cols = lax.dynamic_slice_in_dim(vir_energy, col_pos * block_b, block_b)

time: 468 us -> 440 us (0.940)
  the two profiles are of different devices: /device:TPU:29 before, /device:TPU:13 now
where the time goes in v2:
time: 440 us; the launch traced here: 439 us
  waiting for transfers between devices  253 us (58%)
  matrix products  68.3 us (16%)
  local copies, waits for them, and re-layouts  62.5 us (14%)
  starting transfers between devices  27.3 us (6%)
  between operations  13.7 us (3%)
  Pallas kernels  10.3 us (2%)
    ppermute x6, waiting for transfers between devices, hop(): return lax.ppermute(x, 'col', [(q, q ^ bits) for q in range(cols)])  111 us
    all_gather x2, waiting for transfers between devices, local(): lax.all_gather(planes(ints[:, first:first + width]), 'row', axis=2, tiled...  96.8 us
    dot_general x3, matrix products, local(): jnp.einsum('ikac,kjcb->jiab', amp_all, blocks[:, first - begin:first - be...  57.9 us
    unnamed x32, local copies, waits for them, and re-layouts  21.9 us
    dynamic_update_slice x7, local copies, waits for them, and re-layouts, local(): amp_all = lax.dynamic_update_slice(amp_all, part, (n * HALF, 0, 0, place))  20.7 us
    ppermute x4, waiting for transfers between devices, to_mirror(): arrivals.append(lax.ppermute(moved, ('row', 'col'), along))  19.8 us
    ppermute x3, waiting for transfers between devices, to_mirror(): arrivals = [lax.ppermute(x, ('row', 'col'), direct)]  13.6 us
    ppermute x4, waiting for transfers between devices, to_mirror(): moved = lax.ppermute(x, ('row', 'col'), across)  10.4 us
  transfers between devices with their start and end apart: 22, of which 9 were waited for; matrix products, arithmetic and copies ran while one was open for 24% of the time, Pallas kernels for 2%

profile of v2, /device:TPU:13, one launch (start us, length us, event | category | flops | bytes accessed | tf_op | source)
XLA Modules:
  0.0 438.9 jit_solution(5976115607275338952)
XLA Ops:
  6.5 6.6 %copy.7 = bf16[64,128,256]{1,0,2:T(8,128)(2,1)} copy(bf16[64,128,256]{2,1,0:T(8,128)(2,1)} %param.6) | data formatting | bytes 8388608 | tf_op args[1]
  13.1 5.1 %slice.26 = bf16[16,14,64,128]{3,2,1,0:T(8,128)(2,1)} slice(bf16[16,16,64,128]{3,2,1,0:T(8,128)(2,1)} %bitcast.52), slice={[0:16], [0:14], [0:64], [0:128]} | slice | bytes 7340032 | tf_op jit(solution)/shard_map/slice | solution.py:118
  18.3 6.5 %copy.6 = bf16[64,128,256]{1,0,2:T(8,128)(2,1)} copy(bf16[64,128,256]{2,1,0:T(8,128)(2,1)} %param.5) | data formatting | bytes 8388608 | tf_op args[0]
  24.7 6.0 %fusion.28 = (bf16[8,16,64,128]{3,2,1,0:T(8,128)(2,1)}, bf16[8,16,64,128]{3,2,1,0:T(8,128)(2,1)}) fusion(bf16[16,16,64,128]{3,2,1,0:T(8,128)(2,1)} %bitcast.50), kind=kLoop, calls=%fused_computation.29 | loop fusion | bytes 8388608 | tf_op jit(solution)/shard_map/slice | solution.py:126
  30.8 1.2 collective-permute-start
  32.4 1.3 collective-permute-start.2
  33.7 43.7 %collective-permute-done = bf16[8,16,64,128]{3,2,1,0:T(8,128)(2,1)} collective-permute-done((bf16[8,16,64,128]{3,2,1,0:T(8,128)(2,1)}, bf16[8,16,64,128]{3,2,1,0:T(8,128)(2,1)}, u32[]{:S(2)}, u32[]{:S(2)}) %collective-permute-start) | collective-permute-done | bytes 2097184 | tf_op jit(solution)/shard_map/ppermute | solution.py:124
  78.9 1.9 slice.28
  80.8 6.8 %broadcast_in_dim.2 = bf16[16,16,64,512]{3,2,1,0:T(8,128)(2,1)} broadcast(bf16[]{:T(256)} %constant.31.clone.1), dimensions={} | broadcast | bytes 16777218 | tf_op jit(solution)/shard_map/broadcast_in_dim | solution.py:133
  87.6 3.1 constant_dynamic-update-slice_fusion.6
  90.7 3.2 constant_dynamic-update-slice_fusion.5
  93.9 28.5 %collective-permute-done.1 = bf16[8,16,64,128]{3,2,1,0:T(8,128)(2,1)} collective-permute-done((bf16[8,16,64,128]{3,2,1,0:T(8,128)(2,1)}, bf16[8,16,64,128]{3,2,1,0:T(8,128)(2,1)}, u32[]{:S(2)}, u32[]{:S(2)}) %collective-permute-start.1) | collective-permute-done | bytes 2097184 | tf_op jit(solution)/shard_map/ppermute | solution.py:124
  122.4 3.2 constant_dynamic-update-slice_fusion.4
  125.6 3.2 constant_dynamic-update-slice_fusion.3
  128.8 1.7 constant_dynamic-update-slice_fusion.2
  130.5 37.8 %collective-permute-done.4 = bf16[8,16,64,128]{3,2,1,0:T(8,128)(2,1)} collective-permute-done((bf16[8,16,64,128]{3,2,1,0:T(8,128)(2,1)}, bf16[8,16,64,128]{3,2,1,0:T(8,128)(2,1)}, u32[]{:S(2)}, u32[]{:S(2)}) %collective-permute-start.4) | collective-permute-done | bytes 2097184 | tf_op jit(solution)/shard_map/ppermute | solution.py:124
  168.3 3.1 constant_dynamic-update-slice_fusion.1
  171.4 3.2 constant_dynamic-update-slice_fusion
  174.6 96.8 %all-gather.3.cloned.1.call-done = bf16[16,14,512,128]{3,2,1,0:T(8,128)(2,1)} async-done(((bf16[16,14,64,128]{3,2,1,0:T(8,128)(2,1)}), bf16[16,14,512,128]{3,2,1,0:T(8,128)(2,1)}) %all-gather.3.cloned.1.call-update) | async-done | bytes 29360144 | tf_op jit(solution)/shard_map/all_gather | solution.py:118
  271.4 31.0 %fusion.13.refs_0_.refs_1_ = f32[11,16,64,128]{3,2,1,0:T(8,128)S(1)} fusion(bf16[16,16,64,512]{3,2,1,0:T(8,128)(2,1)} %constant_dynamic-update-slice_fusion, bf16[16,14,512,128]{3,2,1,0:T(8,128)(2,1)} %all-gather.3.cloned.1.call-done), kind=kOutput, calls=%fused_computation.15 | convolution fusion | flops 23622320128 | bytes 45613056 | tf_op jit(solution)/shard_map/ikac,kjcb->jiab/dot_general | solution.py:159
  302.8 1.4 copy-done.2
  304.3 1.6 collective-permute-start.9
  305.8 1.6 collective-permute-start.6
  307.4 3.8 collective-permute-start.7
  311.2 14.5 %fusion.18.refs_0_.refs_2_ = f32[3,16,64,128]{3,2,1,0:T(8,128)S(1)} fusion(bf16[16,16,64,512]{3,2,1,0:T(8,128)(2,1)} %constant_dynamic-update-slice_fusion, bf16[16,14,512,128]{3,2,1,0:T(8,128)(2,1)} %all-gather.3.cloned.1.call-done), kind=kOutput, calls=%fused_computation.16 | convolution fusion | flops 6442450944 | bytes 24641536 | tf_op jit(solution)/shard_map/ikac,kjcb->jiab/dot_general | solution.py:159
  327.8 1.5 collective-permute-start.15
  329.2 2.1 collective-permute-start.13
  331.4 1.5 collective-permute-start.12
  332.9 10.4 %collective-permute-done.13 = bf16[36,64,128]{2,1,0:T(8,128)(2,1)} collective-permute-done((bf16[36,64,128]{2,1,0:T(8,128)(2,1)}, bf16[36,64,128]{2,1,0:T(8,128)(2,1)}, u32[]{:S(2)}, u32[]{:S(2)}) %collective-permute-start.13) | collective-permute-done | bytes 589856 | tf_op jit(solution)/shard_map/ppermute | solution.py:149
  343.3 1.3 collective-permute-start.16
  344.6 1.5 collective-permute-start.14
  346.1 1.3 collective-permute-start.10
  347.4 1.6 collective-permute-start.8
  349.0 12.5 %fusion.23.refs_0_ = f32[2,16,64,128]{3,2,1,0:T(8,128)} fusion(bf16[16,16,64,512]{3,2,1,0:T(8,128)(2,1)} %constant_dynamic-update-slice_fusion, bf16[16,2,512,128]{3,2,1,0:T(8,128)(2,1)} %all-gather.5.cloned.1.call-done), kind=kOutput, calls=%fused_computation.17 | convolution fusion | flops 4294967296 | bytes 22020096 | tf_op jit(solution)/shard_map/ikac,kjcb->jiab/dot_general | solution.py:159
  361.5 2.6 copy-done.1
  365.7 19.8 %collective-permute-done.10 = bf16[55,64,128]{2,1,0:T(8,128)(2,1)S(1)} collective-permute-done((bf16[55,64,128]{2,1,0:T(8,128)(2,1)}, bf16[55,64,128]{2,1,0:T(8,128)(2,1)S(1)}, u32[]{:S(2)}, u32[]{:S(2)}) %collective-permute-start.10) | collective-permute-done | bytes 901152 | tf_op jit(solution)/shard_map/ppermute | solution.py:150
  385.4 2.1 collective-permute-start.18
  387.6 1.8 add_add_fusion.near_ref
  389.4 1.8 collective-permute-start.11
  391.2 1.5 add_add_fusion.1.near_ref
  392.8 13.6 %collective-permute-done.18.near_ref = bf16[29,64,128]{2,1,0:T(8,128)(2,1)} collective-permute-done((bf16[29,64,128]{2,1,0:T(8,128)(2,1)S(1)}, bf16[29,64,128]{2,1,0:T(8,128)(2,1)}, u32[]{:S(2)}, u32[]{:S(2)}) %collective-permute-start.18) | collective-permute-done | bytes 475168 | tf_op jit(solution)/shard_map/ppermute | solution.py:145
  406.5 2.0 collective-permute-start.19
  408.9 1.4 collective-permute-done.19.far_ref
  411.5 2.4 shard_map.60
  413.9 1.3 copy-done.5
  415.2 2.5 shard_map.58
  417.8 3.6 shard_map.56
  421.7 10.3 %divide_add_fusion = f32[64,128,256]{2,1,0:T(8,128)} fusion(bf16[64,128,256]{2,1,0:T(8,128)(2,1)S(1)} %copy-done.10, f32[128]{0:T(128)S(1)} %dynamic_slice.7, f32[64,256]{1,0:T(8,128)S(1)} %broadcast_subtract_fusion, f32[120,256,1]{1,0,2:T(8,128)S(1)} %copy-done.14, f32[64,128,120]{1,0,2:T(8,128)S(1)} %maximum_bitcast_fusion), kind=kOutput, calls=%fused_computation.8 | convolution fusion | flops 1518338048 | bytes 16704000 | tf_op jit(solution)/shard_map/abp,pq->abq/dot_general | solution.py:177
  (59 shorter events, 8.0 us)
Async XLA Ops:
  6.5 264.9 %all-gather.3.cloned.1.call-start = ((), (), s32[]{:S(2)}) async-start(), calls=%async_computation | async-start | bytes 33030144 | tf_op jit(solution)/shard_map/all_gather | solution.py:118
  18.2 313.1 %all-gather.5.cloned.1.call-start = ((), (), s32[]{:S(2)}) async-start(), calls=%async_computation.1 | async-start | bytes 4718592 | tf_op jit(solution)/shard_map/all_gather | solution.py:118
  30.8 46.7 %collective-permute-start = (bf16[8,16,64,128]{3,2,1,0:T(8,128)(2,1)}, bf16[8,16,64,128]{3,2,1,0:T(8,128)(2,1)}, u32[]{:S(2)}, u32[]{:S(2)}) collective-permute-start(bf16[8,16,64,128]{3,2,1,0:T(8,128)(2,1)} %get-tuple-element.22), channel_id=1, source_target_pairs={{0,1},{1,0},{2,3},{3,2},{4,5},{5,4},{6,7},{7,6},{8,9},{9,8},{10,11... | collective-permute-start | bytes 6291464 | tf_op jit(solution)/shard_map/ppermute | solution.py:124
  32.0 46.4 %collective-permute-start.3 = (bf16[8,16,64,128]{3,2,1,0:T(8,128)(2,1)}, bf16[8,16,64,128]{3,2,1,0:T(8,128)(2,1)S(1)}, u32[]{:S(2)}, u32[]{:S(2)}) collective-permute-start(bf16[8,16,64,128]{3,2,1,0:T(8,128)(2,1)} %get-tuple-element.21), channel_id=1, source_target_pairs={{0,2},{1,3},{2,0},{3,1},{4,6},{5,7},{6,4},{7,5},{8,10},{9,11},{10,... | collective-permute-start | bytes 6291464 | tf_op jit(solution)/shard_map/ppermute | solution.py:124
  32.2 90.2 %collective-permute-start.1 = (bf16[8,16,64,128]{3,2,1,0:T(8,128)(2,1)}, bf16[8,16,64,128]{3,2,1,0:T(8,128)(2,1)}, u32[]{:S(2)}, u32[]{:S(2)}) collective-permute-start(bf16[8,16,64,128]{3,2,1,0:T(8,128)(2,1)} %get-tuple-element.21), channel_id=1, source_target_pairs={{0,1},{1,0},{2,3},{3,2},{4,5},{5,4},{6,7},{7,6},{8,9},{9,8},{10,11... | collective-permute-start | bytes 6291464 | tf_op jit(solution)/shard_map/ppermute | solution.py:124
  32.4 93.2 %collective-permute-start.2 = (bf16[8,16,64,128]{3,2,1,0:T(8,128)(2,1)}, bf16[8,16,64,128]{3,2,1,0:T(8,128)(2,1)}, u32[]{:S(2)}, u32[]{:S(2)}) collective-permute-start(bf16[8,16,64,128]{3,2,1,0:T(8,128)(2,1)} %get-tuple-element.22), channel_id=1, source_target_pairs={{0,2},{1,3},{2,0},{3,1},{4,6},{5,7},{6,4},{7,5},{8,10},{9,11},{10,... | collective-permute-start | bytes 6291464 | tf_op jit(solution)/shard_map/ppermute | solution.py:124
  77.5 90.8 %collective-permute-start.4 = (bf16[8,16,64,128]{3,2,1,0:T(8,128)(2,1)}, bf16[8,16,64,128]{3,2,1,0:T(8,128)(2,1)}, u32[]{:S(2)}, u32[]{:S(2)}) collective-permute-start(bf16[8,16,64,128]{3,2,1,0:T(8,128)(2,1)} %collective-permute-done), channel_id=1, source_target_pairs={{0,2},{1,3},{2,0},{3,1},{4,6},{5,7},{6,4},{7,5},{8,10},{9,11},{10,... | collective-permute-start | bytes 6291464 | tf_op jit(solution)/shard_map/ppermute | solution.py:124
  78.4 93.0 %collective-permute-start.5 = (bf16[8,16,64,128]{3,2,1,0:T(8,128)(2,1)S(1)}, bf16[8,16,64,128]{3,2,1,0:T(8,128)(2,1)}, u32[]{:S(2)}, u32[]{:S(2)}) collective-permute-start(bf16[8,16,64,128]{3,2,1,0:T(8,128)(2,1)S(1)} %collective-permute-done.3), channel_id=1, source_target_pairs={{0,1},{1,0},{2,3},{3,2},{4,5},{5,4},{6,7},{7,6},{8,9},{9,8},{10,11... | collective-permute-start | bytes 6291464 | tf_op jit(solution)/shard_map/ppermute | solution.py:124
  80.8 6.8 %copy-start.9 = (bf16[64,128,256]{1,0,2:T(8,128)(2,1)S(1)}, bf16[64,128,256]{1,0,2:T(8,128)(2,1)}, u32[]{:S(2)}) copy-start(bf16[64,128,256]{1,0,2:T(8,128)(2,1)} %copy.6) | copy-start | bytes 12582916
  302.4 23.3 %copy-start = (f32[11,16,64,128]{3,2,1,0:T(8,128)}, f32[11,16,64,128]{3,2,1,0:T(8,128)S(1)}, u32[]{:S(2)}) copy-start(f32[11,16,64,128]{3,2,1,0:T(8,128)S(1)} %fusion.13.refs_0_.refs_1_) | copy-start | bytes 17301508
  302.8 1.5 copy-start.2
  304.3 40.3 %collective-permute-start.9 = (bf16[55,64,128]{2,1,0:T(8,128)(2,1)S(1)}, bf16[55,64,128]{2,1,0:T(8,128)(2,1)}, u32[]{:S(2)}, u32[]{:S(2)}) collective-permute-start(bf16[55,64,128]{2,1,0:T(8,128)(2,1)S(1)} %get-tuple-element.14), channel_id=1, source_target_pairs={{8,9},{12,13},{17,18},{21,22}} | collective-permute-start | bytes 2703368 | tf_op jit(solution)/shard_map/ppermute | solution.py:149
  305.8 40.2 %collective-permute-start.6 = (bf16[55,64,128]{2,1,0:T(8,128)(2,1)S(1)}, bf16[55,64,128]{2,1,0:T(8,128)(2,1)}, u32[]{:S(2)}, u32[]{:S(2)}) collective-permute-start(bf16[55,64,128]{2,1,0:T(8,128)(2,1)S(1)} %get-tuple-element.14), channel_id=1, source_target_pairs={{0,0},{1,8},{2,16},{4,4},{5,12},{6,20},{9,9},{11,25},{13,13},{15,2... | collective-permute-start | bytes 2703368 | tf_op jit(solution)/shard_map/ppermute | solution.py:145
  307.4 40.0 %collective-permute-start.7 = (bf16[55,64,128]{2,1,0:T(8,128)(2,1)S(1)}, bf16[55,64,128]{2,1,0:T(8,128)(2,1)}, u32[]{:S(2)}, u32[]{:S(2)}) collective-permute-start(bf16[55,64,128]{2,1,0:T(8,128)(2,1)S(1)} %get-tuple-element.14), channel_id=1, source_target_pairs={{3,0},{7,4},{10,9},{14,13},{19,18},{23,22},{24,27},{28,31}} | collective-permute-start | bytes 2703368 | tf_op jit(solution)/shard_map/ppermute | solution.py:149
  326.7 1.0 copy-start.4
  327.8 3.6 collective-permute-start.15
  329.2 14.0 %collective-permute-start.13 = (bf16[36,64,128]{2,1,0:T(8,128)(2,1)}, bf16[36,64,128]{2,1,0:T(8,128)(2,1)}, u32[]{:S(2)}, u32[]{:S(2)}) collective-permute-start(bf16[36,64,128]{2,1,0:T(8,128)(2,1)} %get-tuple-element.17), channel_id=1, source_target_pairs={{3,0},{7,4},{10,9},{14,13},{19,18},{23,22},{24,27},{28,31}} | collective-permute-start | bytes 1769480 | tf_op jit(solution)/shard_map/ppermute | solution.py:149
  331.4 59.9 %collective-permute-start.12 = (bf16[36,64,128]{2,1,0:T(8,128)(2,1)}, bf16[36,64,128]{2,1,0:T(8,128)(2,1)}, u32[]{:S(2)}, u32[]{:S(2)}) collective-permute-start(bf16[36,64,128]{2,1,0:T(8,128)(2,1)} %get-tuple-element.17), channel_id=1, source_target_pairs={{0,0},{1,8},{2,16},{4,4},{5,12},{6,20},{9,9},{11,25},{13,13},{15,2... | collective-permute-start | bytes 1769480 | tf_op jit(solution)/shard_map/ppermute | solution.py:145
  343.3 47.9 %collective-permute-start.16 = (bf16[36,64,128]{2,1,0:T(8,128)(2,1)}, bf16[36,64,128]{2,1,0:T(8,128)(2,1)}, u32[]{:S(2)}, u32[]{:S(2)}) collective-permute-start(bf16[36,64,128]{2,1,0:T(8,128)(2,1)} %collective-permute-done.15), channel_id=1, source_target_pairs={{9,1},{13,5},{18,10},{22,14}} | collective-permute-start | bytes 1769480 | tf_op jit(solution)/shard_map/ppermute | solution.py:150
  344.6 46.7 %collective-permute-start.14 = (bf16[36,64,128]{2,1,0:T(8,128)(2,1)}, bf16[36,64,128]{2,1,0:T(8,128)(2,1)}, u32[]{:S(2)}, u32[]{:S(2)}) collective-permute-start(bf16[36,64,128]{2,1,0:T(8,128)(2,1)} %collective-permute-done.13), channel_id=1, source_target_pairs={{0,24},{4,28},{9,17},{13,21},{18,26},{22,30},{27,3},{31,7}} | collective-permute-start | bytes 1769480 | tf_op jit(solution)/shard_map/ppermute | solution.py:150
  346.1 39.3 %collective-permute-start.10 = (bf16[55,64,128]{2,1,0:T(8,128)(2,1)}, bf16[55,64,128]{2,1,0:T(8,128)(2,1)S(1)}, u32[]{:S(2)}, u32[]{:S(2)}) collective-permute-start(bf16[55,64,128]{2,1,0:T(8,128)(2,1)} %collective-permute-done.9), channel_id=1, source_target_pairs={{9,1},{13,5},{18,10},{22,14}} | collective-permute-start | bytes 2703368 | tf_op jit(solution)/shard_map/ppermute | solution.py:150
  347.4 40.2 %collective-permute-start.8 = (bf16[55,64,128]{2,1,0:T(8,128)(2,1)}, bf16[55,64,128]{2,1,0:T(8,128)(2,1)}, u32[]{:S(2)}, u32[]{:S(2)}) collective-permute-start(bf16[55,64,128]{2,1,0:T(8,128)(2,1)} %collective-permute-done.7), channel_id=1, source_target_pairs={{0,24},{4,28},{9,17},{13,21},{18,26},{22,30},{27,3},{31,7}} | collective-permute-start | bytes 2703368 | tf_op jit(solution)/shard_map/ppermute | solution.py:150
  361.5 2.6 copy-start.1
  364.1 1.2 copy-start.6
  365.4 43.2 %copy-start.13 = (f32[512]{0:T(512)S(1)}, f32[512]{0:T(512)}, u32[]{:S(2)}) copy-start(f32[512]{0:T(512)} %param.8) | copy-start | bytes 6148
  365.4 43.3 %copy-start.12 = (f32[16]{0:T(128)S(1)}, f32[16]{0:T(128)}, u32[]{:S(2)}) copy-start(f32[16]{0:T(128)} %param.7) | copy-start | bytes 196
  365.6 25.6 %copy-start.7 = (f32[29,64,128]{2,1,0:T(8,128)}, f32[29,64,128]{2,1,0:T(8,128)S(1)}, u32[]{:S(2)}) copy-start(f32[29,64,128]{2,1,0:T(8,128)S(1)} %get-tuple-element.19.diff_ref) | copy-start | bytes 2850820
  365.6 52.1 %copy-start.3 = (f32[55,64,128]{2,1,0:T(8,128)S(1)}, f32[55,64,128]{2,1,0:T(8,128)}, u32[]{:S(2)}) copy-start(f32[55,64,128]{2,1,0:T(8,128)} %copy-done.2) | copy-start | bytes 5406724
  385.4 2.1 copy-start.11
  385.4 21.1 %collective-permute-start.18 = (bf16[29,64,128]{2,1,0:T(8,128)(2,1)S(1)}, bf16[29,64,128]{2,1,0:T(8,128)(2,1)}, u32[]{:S(2)}, u32[]{:S(2)}) collective-permute-start(bf16[29,64,128]{2,1,0:T(8,128)(2,1)S(1)} %get-tuple-element.20), channel_id=1, source_target_pairs={{0,0},{1,8},{2,16},{3,24},{4,4},{5,12},{6,20},{7,28},{8,1},{9,9},{... | collective-permute-start | bytes 1425416 | tf_op jit(solution)/shard_map/ppermute | solution.py:145
  389.4 28.3 %collective-permute-start.11 = (bf16[55,64,128]{2,1,0:T(8,128)(2,1)S(1)}, bf16[55,64,128]{2,1,0:T(8,128)(2,1)}, u32[]{:S(2)}, u32[]{:S(2)}) collective-permute-start(bf16[55,64,128]{2,1,0:T(8,128)(2,1)S(1)} %add_add_fusion.near_ref), channel_id=1, source_target_pairs={{0,4},{4,0},{8,12},{12,8},{16,20},{20,16},{24,28},{28,24},{1,5},{5... | collective-permute-start | bytes 2703368 | tf_op jit(solution)/shard_map/ppermute | solution.py:109
  392.7 21.2 %collective-permute-start.17 = (bf16[36,64,128]{2,1,0:T(8,128)(2,1)S(1)}, bf16[36,64,128]{2,1,0:T(8,128)(2,1)}, u32[]{:S(2)}, u32[]{:S(2)}) collective-permute-start(bf16[36,64,128]{2,1,0:T(8,128)(2,1)S(1)} %add_add_fusion.1.near_ref), channel_id=1, source_target_pairs={{0,4},{4,0},{8,12},{12,8},{16,20},{20,16},{24,28},{28,24},{1,5},{5... | collective-permute-start | bytes 1769480 | tf_op jit(solution)/shard_map/ppermute | solution.py:109
  406.5 3.9 collective-permute-start.19
  410.3 1.2 copy-start.8
  413.9 1.3 copy-start.5
  417.7 4.0 copy-start.10
  417.8 4.0 copy-start.14
Sparse Core Ops, SparseCore 0:
  18.4 252.9 all-gather.2
  273.0 50.8 all-gather.4
